TPU v7x, 256 devices: a whole 4x4x8 slice. The times are simulated.
256 devices in a mesh: gx: 16 (over z, x_hi), gy: 16 (over y, x_lo, core).
Axes of the slice: x: 4 (x_hi: 2, x_lo: 2; x = x_hi * 2 + x_lo), y: 4, z: 8, core: 2. Of those that a mesh axis runs over, the one named last changes fastest.
Arguments:
- f_in: float32 [19, 16, 256, 2048], P(None, None, 'gx', 'gy')
- rotor_place: int32 [40, 3], replicated, may hold values from 0 to 15, as said below
- marker_cell: int32 [40, 8192], replicated, may hold values from 16384 to 2078527, as said below
- pitch_phase: int32 [40, 2], replicated, may hold values from 0 to 63
- blade_area: float32 [16, 16, 2, 8192], P('gx', 'gy'), may hold values from 0.3 to 1.2
- blade_twist: float32 [16, 16, 2, 8192], P('gx', 'gy'), may hold values from -0.6 to 0.6
- blade_speed: float32 [16, 16, 2, 8192], P('gx', 'gy'), may hold values from 1.5 to 3
- blade_angle: float32 [16, 16, 2, 8192], P('gx', 'gy'), may hold values from -3.14 to 3.14, as said below
- filt_in: float32 [16, 16, 2, 3, 8192], P('gx', 'gy'), may hold values from -1.5 to 1.5
Outputs:
- f_out: float32 [19, 16, 256, 2048], P(None, None, 'gx', 'gy')
- loads_out: float32 [16, 16, 2, 3, 8192], P('gx', 'gy')
- filt_out: float32 [16, 16, 2, 3, 8192], P('gx', 'gy')
Inputs may be any that keep to these rules, and one draw needn't show every extreme that they name: `rotor_place`: column 0 is a streamwise tile holding at most 3 rotors, some exactly 3; column 1 a plane 0 to 15; column 2 the owner's spanwise tile. Every streamwise tile holds 2 or more rotors; one owner holds at most 2 rotors, exactly 2 in every streamwise tile. `marker_cell`: all stencil cells of one rotor lie within two neighbouring spanwise tiles and within levels 0 to 15; a rotor's stencils may cover one or two tiles. `blade_angle`: azimuths in radians.
All inputs are finite; a program needn't handle non-finite values.
Results may differ from a plain program's by a relative error of at most 0.0003.
Values sent between devices are 32-bit elements; how exact they have to be, the bound alone decides.
A program may use at most 128 MiB of HBM per device.

v0:
```python
import math
import jax
import jax.numpy as jnp
import numpy as np
from jax import lax
from jax.sharding import PartitionSpec as P

PHASES = 64
LATTICE_DIRS = np.array(
    [
        [0, 0, 0],
        [1, 0, 0],
        [-1, 0, 0],
        [0, 1, 0],
        [0, -1, 0],
        [0, 0, 1],
        [0, 0, -1],
        [1, 1, 0],
        [-1, -1, 0],
        [1, -1, 0],
        [-1, 1, 0],
        [1, 0, 1],
        [-1, 0, -1],
        [1, 0, -1],
        [-1, 0, 1],
        [0, 1, 1],
        [0, -1, -1],
        [0, 1, -1],
        [0, -1, 1],
    ]
)
OPPOSITE = [0, 2, 1, 4, 3, 6, 5, 8, 7, 10, 9, 12, 11, 14, 13, 16, 15, 18, 17]
LATTICE_WEIGHTS = np.array([1.0 / 3.0] + [1.0 / 18.0] * 6 + [1.0 / 36.0] * 12)
OMEGA = 1.0 / 0.6
SPREAD = 0.01
MIX = 0.5
PITCH_AMP = 0.2


def extended(block, sides, width):
    for axis, dim in sides:
        count = lax.axis_size(axis)
        forward = [(i, i + 1) for i in range(count - 1)]
        forward.append((count - 1, 0))
        backward = [(target, source) for source, target in forward]
        low = lax.ppermute(
            lax.slice_in_dim(block, block.shape[dim] - width, None, axis=dim), axis, forward
        )
        high = lax.ppermute(lax.slice_in_dim(block, 0, width, axis=dim), axis, backward)
        block = jnp.concatenate([low, block, high], axis=dim)
    return block


def peskin(offsets):
    distance = jnp.abs(offsets)
    near_arg = jnp.maximum(1.0 + 4.0 * distance - 4.0 * distance * distance, 1.0)
    far_arg = jnp.maximum(-7.0 + 12.0 * distance - 4.0 * distance * distance, 1.0)
    near_part = (3.0 - 2.0 * distance + jnp.sqrt(near_arg)) / 8.0
    far_part = (5.0 - 2.0 * distance - jnp.sqrt(far_arg)) / 8.0
    return jnp.where(distance <= 1.0, near_part, far_part)


def dense_rows(anchor, weights, width, start):
    column = jnp.arange(width, dtype=jnp.int32)[None, :] + start
    gap = column - anchor[:, None]
    summed = jnp.zeros(gap.shape, jnp.float32)
    for corner in range(4):
        summed = summed + jnp.where(gap == corner, weights[corner][:, None], 0.0)
    return summed


def stencil_tables(cell_codes, levels, width, start):
    fraction_z = (cell_codes % 8).astype(jnp.float32) / 8.0
    fraction_y = (cell_codes // 8 % 8).astype(jnp.float32) / 8.0
    cell_z = cell_codes // 64 % levels
    cell_y = cell_codes // (64 * levels)
    weights_y = [peskin(corner - 1.0 - fraction_y) for corner in range(4)]
    weights_z = [peskin(corner - 1.0 - fraction_z) for corner in range(4)]
    across = dense_rows(cell_y, weights_y, width, start)
    upward = dense_rows(cell_z, weights_z, levels, jnp.int32(0))
    return (across, upward)


def sample_section(section, across, upward):
    levels = section.shape[1]
    width = section.shape[2]
    flattened = jnp.transpose(section, (2, 0, 1)).reshape(width, 3 * levels)
    partial_value = jnp.dot(
        across, flattened, precision=lax.Precision.HIGHEST, preferred_element_type=jnp.float32
    )
    partial_value = partial_value.reshape(across.shape[0], 3, levels)
    return jnp.transpose(jnp.sum(partial_value * upward[:, None, :], axis=2))


def spread_section(marker_loads, across, upward):
    markers = upward.shape[0]
    levels = upward.shape[1]
    weighted = (upward[:, None, :] * jnp.transpose(marker_loads)[:, :, None]).reshape(
        markers, 3 * levels
    )
    section = lax.dot_general(
        weighted,
        across,
        (((0,), (0,)), ((), ())),
        precision=lax.Precision.HIGHEST,
        preferred_element_type=jnp.float32,
    )
    return -SPREAD * section.reshape(3, levels, across.shape[1])


def pitch_angles(phases):
    return PITCH_AMP * jnp.sin(2.0 * math.pi * phases.astype(jnp.float32) / PHASES)


def blade_loads(filtered, area, twist, speed, angle, pitch):
    axial_speed = filtered[..., 0, :]
    sin_t = jnp.sin(angle)
    cos_t = jnp.cos(angle)
    tangent = speed + sin_t * filtered[..., 1, :] - cos_t * filtered[..., 2, :]
    square = axial_speed * axial_speed + tangent * tangent
    magnitude = jnp.sqrt(square)
    sin_p = axial_speed / magnitude
    cos_p = tangent / magnitude
    blade_pitch = twist + pitch
    sin_a = sin_p * jnp.cos(blade_pitch) - cos_p * jnp.sin(blade_pitch)
    cos_a = cos_p * jnp.cos(blade_pitch) + sin_p * jnp.sin(blade_pitch)
    lift_coef = 2.0 * math.pi * sin_a * cos_a
    drag_coef = 0.02 + sin_a * sin_a
    dynamic = 0.5 * area * square
    normal = dynamic * (lift_coef * cos_p + drag_coef * sin_p)
    tangential = dynamic * (lift_coef * sin_p - drag_coef * cos_p)
    return jnp.stack([normal, -tangential * sin_t, tangential * cos_t], axis=-2)


def velocity(populations):
    lattice = jnp.asarray(LATTICE_DIRS, jnp.float32)
    density = jnp.sum(populations, axis=0)
    parts = [
        jnp.sum(populations * lattice[:, axis][:, None, None, None], axis=0) / density
        for axis in range(3)
    ]
    return jnp.stack(parts)


def collide(populations, force_field):
    lattice = jnp.asarray(LATTICE_DIRS, jnp.float32)
    weights = jnp.asarray(LATTICE_WEIGHTS, jnp.float32)[:, None, None, None]
    density = jnp.sum(populations, axis=0)
    columns = [lattice[:, axis][:, None, None, None] for axis in range(3)]
    parts = [
        (jnp.sum(populations * columns[axis], axis=0) + 0.5 * force_field[axis]) / density
        for axis in range(3)
    ]
    project = (
        columns[0] * parts[0][None] + columns[1] * parts[1][None] + columns[2] * parts[2][None]
    )
    force_proj = (
        columns[0] * force_field[0][None]
        + columns[1] * force_field[1][None]
        + columns[2] * force_field[2][None]
    )
    speed_sq = parts[0] * parts[0] + parts[1] * parts[1] + parts[2] * parts[2]
    work_rate = parts[0] * force_field[0] + parts[1] * force_field[1] + parts[2] * force_field[2]
    equilibrium = (
        weights
        * density[None]
        * (1.0 + 3.0 * project + 4.5 * project * project - 1.5 * speed_sq[None])
    )
    source = (
        (1.0 - 0.5 * OMEGA)
        * weights
        * (3.0 * (force_proj - work_rate[None]) + 9.0 * project * force_proj)
    )
    return populations - OMEGA * (populations - equilibrium) + source


def stream(padded, collided):
    x_cells = collided.shape[2]
    y_cells = collided.shape[3]
    outgoing = []
    for direction in range(19):
        shift_x = int(LATTICE_DIRS[direction, 0])
        shift_y = int(LATTICE_DIRS[direction, 1])
        shift_z = int(LATTICE_DIRS[direction, 2])
        pulled = padded[
            direction, :, 1 - shift_x : 1 - shift_x + x_cells, 1 - shift_y : 1 - shift_y + y_cells
        ]
        mirror = collided[OPPOSITE[direction]]
        if shift_z == 1:
            pulled = jnp.concatenate([mirror[:1], pulled[:-1]], axis=0)
        elif shift_z == -1:
            pulled = jnp.concatenate([pulled[1:], mirror[-1:]], axis=0)
        outgoing.append(pulled)
    return jnp.stack(outgoing)


def with_ghosts(collided):
    padded = extended(collided, (("gx", 2), ("gy", 3)), 1)
    return padded


def local(
    f_in,
    rotor_place,
    marker_cell,
    pitch_phase,
    blade_area,
    blade_twist,
    blade_speed,
    blade_angle,
    filt_in,
):
    levels = f_in.shape[1]
    x_cells = f_in.shape[2]
    y_cells = f_in.shape[3]
    rotors = rotor_place.shape[0]
    step_count = pitch_phase.shape[1]
    owned_count = filt_in.shape[2]
    spread_x = lax.axis_size("gx")
    row_slots = (rotors + spread_x - 1) // spread_x
    here_x = lax.axis_index("gx")
    here_y = lax.axis_index("gy")
    street = rotor_place[:, 0]
    plane_x = rotor_place[:, 1]
    owner_y = rotor_place[:, 2]
    rotor_ids = jnp.arange(rotors, dtype=jnp.int32)
    earlier = rotor_ids[None, :] < rotor_ids[:, None]
    same_row = street[:, None] == street[None, :]
    row_rank = jnp.sum((earlier & same_row).astype(jnp.int32), axis=1)
    same_owner = same_row & (owner_y[:, None] == owner_y[None, :])
    owner_rank = jnp.sum((earlier & same_owner).astype(jnp.int32), axis=1)
    slot_ids = jnp.arange(row_slots, dtype=jnp.int32)
    slot_pick = ((street[None, :] == here_x) & (row_rank[None, :] == slot_ids[:, None])).astype(
        jnp.int32
    )
    slot_valid = jnp.sum(slot_pick, axis=1)
    slot_rotor = jnp.sum(slot_pick * rotor_ids[None, :], axis=1)
    slot_codes = jnp.take(marker_cell, slot_rotor, axis=0)
    slot_plane = jnp.take(plane_x, slot_rotor)
    slot_pitch = pitch_angles(jnp.take(pitch_phase, slot_rotor, axis=0))
    owned_here = (jnp.take(owner_y, slot_rotor) == here_y) & (slot_valid > 0)
    owned_ids = jnp.arange(owned_count, dtype=jnp.int32)
    own_pick = (
        owned_here[None, :] & (jnp.take(owner_rank, slot_rotor)[None, :] == owned_ids[:, None])
    ).astype(jnp.float32)
    valid_float = slot_valid.astype(jnp.float32)
    start_y = here_y * y_cells
    tables = []
    for slot_index in range(row_slots):
        across, upward = stencil_tables(slot_codes[slot_index], levels, y_cells, start_y)
        tables.append((across * valid_float[slot_index], upward))
    x_ids = jnp.arange(x_cells, dtype=jnp.int32)
    filtered = filt_in[0, 0]
    own_pitch = jnp.sum(own_pick[:, :, None] * slot_pitch[None], axis=1)
    populations = f_in
    for step_index in range(step_count):
        field_speed = velocity(populations)
        samples = jnp.stack(
            [
                sample_section(
                    lax.dynamic_index_in_dim(
                        field_speed, slot_plane[slot_index], 2, keepdims=False
                    ),
                    tables[slot_index][0],
                    tables[slot_index][1],
                )
                for slot_index in range(row_slots)
            ]
        )
        sampled = lax.psum(samples, "gy")
        own_sampled = jnp.sum(own_pick[:, :, None, None] * sampled[None], axis=1)
        filtered = filtered + MIX * (own_sampled - filtered)
        own_loads = blade_loads(
            filtered,
            blade_area[0, 0],
            blade_twist[0, 0],
            blade_speed[0, 0],
            blade_angle[0, 0],
            own_pitch[:, step_index][:, None],
        )
        row_loads = jnp.sum(own_pick[:, :, None, None] * own_loads[:, None], axis=0)
        load_rows = lax.psum(row_loads, "gy")
        force_field = jnp.zeros((3, levels, x_cells, y_cells), jnp.float32)
        for slot_index in range(row_slots):
            section = spread_section(
                load_rows[slot_index], tables[slot_index][0], tables[slot_index][1]
            )
            plane_mask = (x_ids == slot_plane[slot_index]).astype(jnp.float32)
            force_field = force_field + section[:, :, None, :] * plane_mask[None, None, :, None]
        collided = collide(populations, force_field)
        populations = stream(with_ghosts(collided), collided)
    has_rotor = jnp.sum(own_pick, axis=1)[:, None, None]
    loads_out = own_loads * has_rotor
    filt_out = filtered * has_rotor
    return (populations, loads_out[None, None], filt_out[None, None])


def solution(mesh):
    in_specs = (
        P(None, None, "gx", "gy"),
        P(),
        P(),
        P(),
        P("gx", "gy", None, None),
        P("gx", "gy", None, None),
        P("gx", "gy", None, None),
        P("gx", "gy", None, None),
        P("gx", "gy", None, None, None),
    )
    out_specs = (
        P(None, None, "gx", "gy"),
        P("gx", "gy", None, None, None),
        P("gx", "gy", None, None, None),
    )
    return jax.shard_map(local, mesh=mesh, in_specs=in_specs, out_specs=out_specs, check_vma=False)
```

profile of v0, /device:TPU:27, one launch (start us, length us, event | category | flops | bytes accessed | tf_op | source)
XLA Modules:
  0.0 818.9 jit_solution(7639344466328767253)
XLA Ops:
  7.3 0.8 slice_bitcast_fusion.36
  20.0 2.4 multiply_reduce_fusion.5
  23.2 16.3 %fusion.50 = f32[8192,3]{0,1:T(4,128)S(1)} fusion(f32[3,16,128]{2,1,0:T(8,128)S(1)} %bitcast.602, f32[]{:T(128)} %bitcast.34, f32[8192]{0:T(1024)S(1)} %get-tuple-element.179, f32[8192]{0:T(1024)S(1)} %get-tuple-element.178, f32[8192]{0:T(1024)S(1)} %get-tuple-element.177, f32[8192]{0:T(1024)S(1)} %get-tuple-element.175, s32[8192]{0:T(1024)S(1)} %get-tuple-element.170, ...), kind=kOutput, calls=%fused_computation.82 | convolution fusion | flops 618373120 | bytes 811524 | tf_op jit(solution)/shard_map/dot_general | solution.py:88
  39.6 16.2 %fusion.44 = f32[8192,3]{0,1:T(4,128)S(1)} fusion(f32[3,16,128]{2,1,0:T(8,128)S(1)} %bitcast.601, f32[]{:T(128)} %bitcast.8, f32[8192]{0:T(1024)S(1)} %get-tuple-element.157, f32[8192]{0:T(1024)S(1)} %get-tuple-element.156, f32[8192]{0:T(1024)S(1)} %get-tuple-element.155, f32[8192]{0:T(1024)S(1)} %get-tuple-element.153, s32[8192]{0:T(1024)S(1)} %get-tuple-element.148, ...), kind=kOutput, calls=%fused_computation.80 | convolution fusion | flops 618373120 | bytes 811524 | tf_op jit(solution)/shard_map/dot_general | solution.py:88
  56.0 16.4 %fusion.47 = f32[8192,3]{0,1:T(4,128)S(1)} fusion(f32[3,16,128]{2,1,0:T(8,128)S(1)} %bitcast.600, f32[]{:T(128)} %bitcast.23, f32[8192]{0:T(1024)S(1)} %get-tuple-element.168, f32[8192]{0:T(1024)S(1)} %get-tuple-element.167, f32[8192]{0:T(1024)S(1)} %get-tuple-element.166, f32[8192]{0:T(1024)S(1)} %get-tuple-element.164, s32[8192]{0:T(1024)S(1)} %get-tuple-element.159, ...), kind=kOutput, calls=%fused_computation.81 | convolution fusion | flops 618373120 | bytes 811524 | tf_op jit(solution)/shard_map/dot_general | solution.py:88
  72.4 0.8 pad_maximum_fusion.3
  74.8 1.0 fusion.419
  76.9 123.3 %all-reduce.5.cloned.1.call-done = f32[3,3,8192]{2,1,0:T(4,128)} async-done(((f32[3,3,8192]{2,1,0:T(4,128)}), f32[3,3,8192]{2,1,0:T(4,128)}) %all-reduce.5.cloned.1.call-update) | async-done | bytes 294928 | tf_op jit(solution)/shard_map/psum | solution.py:270
  200.2 1.5 multiply_reduce_fusion.9
  201.8 1.4 add_multiply_fusion.17
  203.2 1.4 bitcast_multiply_fusion.3
  204.7 1.6 multiply_reduce_fusion.8
  208.5 122.4 %all-reduce.7.cloned.1.call-done = f32[3,3,8192]{2,1,0:T(4,128)} async-done(((f32[3,3,8192]{2,1,0:T(4,128)}), f32[3,3,8192]{2,1,0:T(4,128)}) %all-reduce.7.cloned.1.call-update) | async-done | bytes 294928 | tf_op jit(solution)/shard_map/psum | solution.py:282
  330.8 1.1 slice_bitcast_fusion.5
  332.0 8.6 %fusion.62 = f32[3,16,128]{2,1,0:T(8,128)S(1)} fusion(f32[]{:T(128)} %bitcast.8, f32[8192]{0:T(1024)} %copy-done.68, f32[8192]{0:T(1024)} %copy-done.66, f32[8192]{0:T(1024)} %copy-done.64, f32[8192]{0:T(1024)S(1)} %copy-done.48, s32[8192]{0:T(1024)S(1)} %get-tuple-element.148, s32[128]{0:T(128)S(1)} %copy-done.120, f32[8192,3]{0,1:T(4,128)S(1)} %get-tuple-element.131, ...), kind=kOutput, calls=%fused_computation.86 | convolution fusion | flops 618010624 | bytes 811524 | tf_op jit(solution)/shard_map/dot_general | solution.py:101
  340.7 7.9 fusion.82
  348.7 8.3 %fusion.72 = f32[3,16,128]{2,1,0:T(8,128)S(1)} fusion(f32[]{:T(128)} %bitcast.23, f32[8192]{0:T(1024)S(1)} %copy-done.77, f32[8192]{0:T(1024)S(1)} %copy-done.74, f32[8192]{0:T(1024)S(1)} %copy-done.71, f32[8192]{0:T(1024)S(1)} %copy-done.54, s32[8192]{0:T(1024)S(1)} %copy-done.51, s32[128]{0:T(128)S(1)} %copy-done.120, ...), kind=kOutput, calls=%fused_computation.88 | convolution fusion | flops 618010624 | bytes 811524 | tf_op jit(solution)/shard_map/dot_general | solution.py:101
  357.4 1.3 copy-done.11
  358.7 2.5 fusion.24
  362.1 4.5 collective-permute-start.1
  367.3 1.5 collective-permute-done.1
  368.9 5.5 collective-permute-done
  375.0 4.4 fusion.415
  379.4 4.1 copy.171
  383.5 4.1 copy.169
  387.6 2.3 collective-permute-start.2
  392.2 4.8 collective-permute-done.3
  396.9 5.9 copy.172
  402.8 5.6 copy.170
  408.4 1.9 constant_dynamic-update-slice_fusion.5
  410.6 0.8 constant_dynamic-update-slice_fusion.4
  412.9 1.4 copy-done.8
  417.6 16.4 %fusion.59 = f32[8192,3]{0,1:T(4,128)S(1)} fusion(f32[3,16,128]{2,1,0:T(8,128)S(1)} %bitcast.605, f32[]{:T(128)} %bitcast.34, f32[8192]{0:T(1024)S(1)} %copy-done.89, f32[8192]{0:T(1024)S(1)} %copy-done.85, f32[8192]{0:T(1024)S(1)} %copy-done.81, f32[8192]{0:T(1024)S(1)} %copy-done.62, s32[8192]{0:T(1024)S(1)} %copy-done.58, s32[128]{0:T(128)S(1)} %copy-done.121, ...), kind=kOutput, calls=%fused_computation.85 | convolution fusion | flops 618373120 | bytes 811524 | tf_op jit(solution)/shard_map/dot_general | solution.py:88
  434.1 16.4 %fusion.56 = f32[8192,3]{0,1:T(4,128)S(1)} fusion(f32[3,16,128]{2,1,0:T(8,128)S(1)} %bitcast.604, f32[]{:T(128)} %bitcast.23, f32[8192]{0:T(1024)S(1)} %copy-done.78, f32[8192]{0:T(1024)S(1)} %copy-done.75, f32[8192]{0:T(1024)S(1)} %copy-done.72, f32[8192]{0:T(1024)S(1)} %copy-done.55, s32[8192]{0:T(1024)S(1)} %copy-done.52, s32[128]{0:T(128)S(1)} %copy-done.121, ...), kind=kOutput, calls=%fused_computation.84 | convolution fusion | flops 618373120 | bytes 811524 | tf_op jit(solution)/shard_map/dot_general | solution.py:88
  450.6 16.3 %fusion.53 = f32[8192,3]{0,1:T(4,128)S(1)} fusion(f32[3,16,128]{2,1,0:T(8,128)S(1)} %bitcast.603, f32[]{:T(128)} %bitcast.8, f32[8192]{0:T(1024)S(1)} %copy-done.69, f32[8192]{0:T(1024)S(1)} %copy-done.67, f32[8192]{0:T(1024)S(1)} %copy-done.65, f32[8192]{0:T(1024)S(1)} %copy-done.49, s32[8192]{0:T(1024)S(1)} %copy-done.46, s32[128]{0:T(128)S(1)} %copy-done.121, ...), kind=kOutput, calls=%fused_computation.83 | convolution fusion | flops 618373120 | bytes 811524 | tf_op jit(solution)/shard_map/dot_general | solution.py:88
  466.9 0.8 pad_maximum_fusion.5
  467.9 121.0 %all-reduce.9.cloned.1.call-done = f32[3,3,8192]{2,1,0:T(4,128)} async-done(((f32[3,3,8192]{2,1,0:T(4,128)}), f32[3,3,8192]{2,1,0:T(4,128)}) %all-reduce.9.cloned.1.call-update) | async-done | bytes 294928 | tf_op jit(solution)/shard_map/psum | solution.py:270
  588.9 1.5 multiply_reduce_fusion.7
  590.5 1.6 add_multiply_fusion.15
  592.1 1.4 bitcast_multiply_fusion.2
  593.6 1.6 multiply_reduce_fusion.6
  595.2 1.0 fusion.118
  596.3 123.5 %all-reduce.11.cloned.1.call-done = f32[3,3,8192]{2,1,0:T(4,128)} async-done(((f32[3,3,8192]{2,1,0:T(4,128)}), f32[3,3,8192]{2,1,0:T(4,128)}) %all-reduce.11.cloned.1.call-update) | async-done | bytes 294928 | tf_op jit(solution)/shard_map/psum | solution.py:282
  719.8 1.1 slice_bitcast_fusion.2
  721.0 8.7 %fusion.77 = f32[3,16,128]{2,1,0:T(8,128)S(1)} fusion(f32[]{:T(128)} %bitcast.23, f32[8192]{0:T(1024)} %copy-done.76, f32[8192]{0:T(1024)} %copy-done.73, f32[8192]{0:T(1024)} %copy-done.70, f32[8192]{0:T(1024)S(1)} %copy-done.55, s32[8192]{0:T(1024)S(1)} %copy-done.52, s32[128]{0:T(128)} %copy-done.119, f32[8192,3]{0,1:T(4,128)S(1)} %get-tuple-element.123, ...), kind=kOutput, calls=%fused_computation.89 | convolution fusion | flops 618010624 | bytes 811524 | tf_op jit(solution)/shard_map/dot_general | solution.py:101
  729.7 7.8 fusion.87
  737.7 8.1 fusion.67
  746.2 1.3 copy-done.10
  747.5 2.5 fusion.31
  750.2 0.9 slice_dynamic-update-slice_fusion
  751.1 4.5 collective-permute-start.5
  755.6 2.2 collective-permute-done.5
  757.8 5.5 collective-permute-done.4
  764.0 4.4 fusion.414
  768.4 4.1 copy.175
  772.5 3.5 copy.173
  775.9 2.7 collective-permute-start.6
  780.1 5.6 collective-permute-done.7
  785.6 5.6 copy.176
  791.3 5.7 copy.174
  797.0 1.9 maximum_dynamic-update-slice_fusion.5
  799.1 0.8 maximum_dynamic-update-slice_fusion.4
  803.1 0.8 maximum_dynamic-update-slice_fusion.2
  803.9 1.9 maximum_dynamic-update-slice_fusion.1
  (361 shorter events, 34.1 us)
Async XLA Ops:
  7.2 192.9 %all-reduce.5.cloned.1.call-start = ((), (), s32[]{:S(2)}) async-start(), calls=%async_computation | async-start | bytes 786432 | tf_op jit(solution)/shard_map/psum | solution.py:270
  16.1 39.8 %copy-start.50 = (s32[8192]{0:T(1024)}, s32[8192]{0:T(1024)S(1)}, u32[]{:S(2)}) copy-start(s32[8192]{0:T(1024)S(1)} %get-tuple-element.159) | copy-start | bytes 98308
  16.3 39.6 %copy-start.53 = (f32[8192]{0:T(1024)}, f32[8192]{0:T(1024)S(1)}, u32[]{:S(2)}) copy-start(f32[8192]{0:T(1024)S(1)} %get-tuple-element.164) | copy-start | bytes 98308
  16.4 315.6 %copy-start.45 = (s32[8192]{0:T(1024)}, s32[8192]{0:T(1024)S(1)}, u32[]{:S(2)}) copy-start(s32[8192]{0:T(1024)S(1)} %get-tuple-element.148) | copy-start | bytes 98308
  16.6 23.0 %copy-start.47 = (f32[8192]{0:T(1024)}, f32[8192]{0:T(1024)S(1)}, u32[]{:S(2)}) copy-start(f32[8192]{0:T(1024)S(1)} %get-tuple-element.153) | copy-start | bytes 98308
  17.0 22.6 %copy-start.60 = (f32[8192]{0:T(1024)}, f32[8192]{0:T(1024)S(1)}, u32[]{:S(2)}) copy-start(f32[8192]{0:T(1024)S(1)} %get-tuple-element.175) | copy-start | bytes 98308
  17.0 38.9 %copy-start.119 = (s32[128]{0:T(128)}, s32[128]{0:T(128)S(1)}, u32[]{:S(2)}) copy-start(s32[128]{0:T(128)S(1)} %iota_add_fusion) | copy-start | bytes 1540
  17.7 38.2 %copy-start.70 = (f32[8192]{0:T(1024)}, f32[8192]{0:T(1024)S(1)}, u32[]{:S(2)}) copy-start(f32[8192]{0:T(1024)S(1)} %get-tuple-element.166) | copy-start | bytes 98308
  17.7 38.2 %copy-start.73 = (f32[8192]{0:T(1024)}, f32[8192]{0:T(1024)S(1)}, u32[]{:S(2)}) copy-start(f32[8192]{0:T(1024)S(1)} %get-tuple-element.167) | copy-start | bytes 98308
  17.7 38.2 %copy-start.76 = (f32[8192]{0:T(1024)}, f32[8192]{0:T(1024)S(1)}, u32[]{:S(2)}) copy-start(f32[8192]{0:T(1024)S(1)} %get-tuple-element.168) | copy-start | bytes 98308
  17.9 21.7 %copy-start.64 = (f32[8192]{0:T(1024)}, f32[8192]{0:T(1024)S(1)}, u32[]{:S(2)}) copy-start(f32[8192]{0:T(1024)S(1)} %get-tuple-element.155) | copy-start | bytes 98308
  17.9 21.7 %copy-start.66 = (f32[8192]{0:T(1024)}, f32[8192]{0:T(1024)S(1)}, u32[]{:S(2)}) copy-start(f32[8192]{0:T(1024)S(1)} %get-tuple-element.156) | copy-start | bytes 98308
  17.9 21.7 %copy-start.68 = (f32[8192]{0:T(1024)}, f32[8192]{0:T(1024)S(1)}, u32[]{:S(2)}) copy-start(f32[8192]{0:T(1024)S(1)} %get-tuple-element.157) | copy-start | bytes 98308
  18.0 21.6 %copy-start.79 = (f32[8192]{0:T(1024)}, f32[8192]{0:T(1024)S(1)}, u32[]{:S(2)}) copy-start(f32[8192]{0:T(1024)S(1)} %get-tuple-element.177) | copy-start | bytes 98308
  18.0 21.6 %copy-start.83 = (f32[8192]{0:T(1024)}, f32[8192]{0:T(1024)S(1)}, u32[]{:S(2)}) copy-start(f32[8192]{0:T(1024)S(1)} %get-tuple-element.178) | copy-start | bytes 98308
  18.0 21.6 %copy-start.87 = (f32[8192]{0:T(1024)}, f32[8192]{0:T(1024)S(1)}, u32[]{:S(2)}) copy-start(f32[8192]{0:T(1024)S(1)} %get-tuple-element.179) | copy-start | bytes 98308
  22.7 317.9 %copy-start.28 = (f32[8192,16]{0,1:T(8,128)}, f32[8192,16]{0,1:T(8,128)S(1)}, u32[]{:S(2)}) copy-start(f32[8192,16]{0,1:T(8,128)S(1)} %select_add_fusion) | copy-start | bytes 1572868
  23.0 309.0 %copy-start.26 = (f32[8192,16]{0,1:T(8,128)}, f32[8192,16]{0,1:T(8,128)S(1)}, u32[]{:S(2)}) copy-start(f32[8192,16]{0,1:T(8,128)S(1)} %select_add_fusion.2) | copy-start | bytes 1572868
  23.2 325.4 %copy-start.31 = (f32[8192,16]{0,1:T(8,128)}, f32[8192,16]{0,1:T(8,128)S(1)}, u32[]{:S(2)}) copy-start(f32[8192,16]{0,1:T(8,128)S(1)} %select_add_fusion.1) | copy-start | bytes 1572868
  56.0 18.1 %copy-start.118 = (s32[40,2]{0,1:T(2,128)S(1)}, s32[40,2]{0,1:T(2,128)}, u32[]{:S(2)}) copy-start(s32[40,2]{0,1:T(2,128)} %param.20) | copy-start | bytes 964
  56.0 18.8 %copy-start.42 = (f32[1,1,2,8192]{3,2,1,0:T(2,128)S(1)}, f32[1,1,2,8192]{3,2,1,0:T(2,128)}, u32[]{:S(2)}) copy-start(f32[1,1,2,8192]{3,2,1,0:T(2,128)} %param.24) | copy-start | bytes 196612
  56.0 19.8 %copy-start.110 = (s32[3]{0:T(128)S(1)}, s32[3]{0:T(128)}, u32[]{:S(2)}) copy-start(s32[3]{0:T(128)} %get-tuple-element.61) | copy-start | bytes 40
  56.0 145.6 %copy-start.22 = (f32[1,1,2,3,8192]{4,2,3,1,0:T(2,128)S(1)}, f32[1,1,2,3,8192]{4,2,3,1,0:T(2,128)}, u32[]{:S(2)}) copy-start(f32[1,1,2,3,8192]{4,2,3,1,0:T(2,128)} %param.25) | copy-start | bytes 589828
  56.0 145.8 %copy-start.19 = (f32[1,1,2,8192]{3,2,1,0:T(2,128)S(1)}, f32[1,1,2,8192]{3,2,1,0:T(2,128)}, u32[]{:S(2)}) copy-start(f32[1,1,2,8192]{3,2,1,0:T(2,128)} %param.22) | copy-start | bytes 196612
  56.0 145.8 %copy-start.20 = (f32[1,1,2,8192]{3,2,1,0:T(2,128)S(1)}, f32[1,1,2,8192]{3,2,1,0:T(2,128)}, u32[]{:S(2)}) copy-start(f32[1,1,2,8192]{3,2,1,0:T(2,128)} %param.21) | copy-start | bytes 196612
  56.0 145.8 %copy-start.33 = (f32[1,1,2,8192]{3,2,1,0:T(2,128)S(1)}, f32[1,1,2,8192]{3,2,1,0:T(2,128)}, u32[]{:S(2)}) copy-start(f32[1,1,2,8192]{3,2,1,0:T(2,128)} %param.23) | copy-start | bytes 196612
  72.4 259.5 %copy-start.48 = (f32[8192]{0:T(1024)S(1)}, f32[8192]{0:T(1024)}, u32[]{:S(2)}) copy-start(f32[8192]{0:T(1024)} %copy-done.47) | copy-start | bytes 98308
  73.3 258.7 %copy-start.120 = (s32[128]{0:T(128)S(1)}, s32[128]{0:T(128)}, u32[]{:S(2)}) copy-start(s32[128]{0:T(128)} %copy-done.119) | copy-start | bytes 1540
  73.3 257.5 %all-reduce.7.cloned.1.call-start = ((), (), s32[]{:S(2)}) async-start(), calls=%async_computation.1 | async-start | bytes 786432 | tf_op jit(solution)/shard_map/psum | solution.py:282
  75.9 264.7 %copy-start.43 = (f32[2,3]{0,1:T(4,128)}, f32[2,3]{0,1:T(4,128)S(1)}, u32[]{:S(2)}) copy-start(f32[2,3]{0,1:T(4,128)S(1)} %copy.166) | copy-start | bytes 76
  206.3 382.6 %all-reduce.9.cloned.1.call-start = ((), (), s32[]{:S(2)}) async-start(), calls=%async_computation.2 | async-start | bytes 786432 | tf_op jit(solution)/shard_map/psum | solution.py:270
  207.2 149.8 %copy-start.112 = (f32[16]{0:T(128)}, f32[16]{0:T(128)S(1)}, u32[]{:S(2)}) copy-start(f32[16]{0:T(128)S(1)} %compare_convert_fusion.2) | copy-start | bytes 196
  207.9 149.2 %copy-start.114 = (f32[16]{0:T(128)}, f32[16]{0:T(128)S(1)}, u32[]{:S(2)}) copy-start(f32[16]{0:T(128)S(1)} %compare_convert_fusion) | copy-start | bytes 196
  208.4 148.6 %copy-start.116 = (f32[16]{0:T(128)}, f32[16]{0:T(128)S(1)}, u32[]{:S(2)}) copy-start(f32[16]{0:T(128)S(1)} %compare_convert_fusion.1) | copy-start | bytes 196
  362.1 6.7 collective-permute-start.1
  366.7 7.7 collective-permute-start
  367.3 48.5 %copy-start.35 = (f32[1,16,128]{2,1,0:T(8,128)}, f32[1,16,128]{2,1,0:T(8,128)S(1)}, u32[]{:S(2)}) copy-start(f32[1,16,128]{2,1,0:T(8,128)S(1)} %get-tuple-element.106) | copy-start | bytes 24580
  387.6 15.2 %collective-permute-start.2 = (f32[19,16,18,1]{0,1,3,2:T(8,128)}, f32[19,16,18,1]{0,1,3,2:T(8,128)}, u32[]{:S(2)}, u32[]{:S(2)}) collective-permute-start(f32[19,16,18,1]{0,1,3,2:T(8,128)} %copy.169), channel_id=1, source_target_pairs={{0,1},{1,2},{2,3},{3,4},{4,5},{5,6},{6,7},{7,8},{8,9},{9,10},{10,1... | collective-permute-start | bytes 65672 | tf_op jit(solution)/shard_map/ppermute | solution.py:46
  389.9 7.0 collective-permute-start.3
  390.7 25.1 %copy-start.14 = (f32[15,16,128]{2,1,0:T(8,128)}, f32[15,16,128]{2,1,0:T(8,128)S(1)}, u32[]{:S(2)}) copy-start(f32[15,16,128]{2,1,0:T(8,128)S(1)} %get-tuple-element.85) | copy-start | bytes 368644
  416.0 18.0 %copy-start.9 = (f32[19,16,16,128]{3,2,1,0:T(8,128)}, f32[19,16,16,128]{3,2,1,0:T(8,128)S(1)}, u32[]{:S(2)}) copy-start(f32[19,16,16,128]{3,2,1,0:T(8,128)S(1)} %fusion.145) | copy-start | bytes 7471108
  416.6 17.3 %copy-start.12 = (f32[16,16,128]{2,1,0:T(8,128)}, f32[16,16,128]{2,1,0:T(8,128)S(1)}, u32[]{:S(2)}) copy-start(f32[16,16,128]{2,1,0:T(8,128)S(1)} %get-tuple-element.12) | copy-start | bytes 393220
  417.5 16.4 %copy-start.52 = (s32[8192]{0:T(1024)S(1)}, s32[8192]{0:T(1024)}, u32[]{:S(2)}) copy-start(s32[8192]{0:T(1024)} %copy-done.50) | copy-start | bytes 98308
  417.5 16.4 %copy-start.55 = (f32[8192]{0:T(1024)S(1)}, f32[8192]{0:T(1024)}, u32[]{:S(2)}) copy-start(f32[8192]{0:T(1024)} %copy-done.53) | copy-start | bytes 98308
  417.5 16.4 %copy-start.72 = (f32[8192]{0:T(1024)S(1)}, f32[8192]{0:T(1024)}, u32[]{:S(2)}) copy-start(f32[8192]{0:T(1024)} %copy-done.70) | copy-start | bytes 98308
  417.6 16.4 %copy-start.75 = (f32[8192]{0:T(1024)S(1)}, f32[8192]{0:T(1024)}, u32[]{:S(2)}) copy-start(f32[8192]{0:T(1024)} %copy-done.73) | copy-start | bytes 98308
  417.6 16.4 %copy-start.78 = (f32[8192]{0:T(1024)S(1)}, f32[8192]{0:T(1024)}, u32[]{:S(2)}) copy-start(f32[8192]{0:T(1024)} %copy-done.76) | copy-start | bytes 98308
  434.0 16.4 %copy-start.27 = (f32[8192,16]{0,1:T(8,128)S(1)}, f32[8192,16]{0,1:T(8,128)}, u32[]{:S(2)}) copy-start(f32[8192,16]{0,1:T(8,128)} %copy-done.26) | copy-start | bytes 1572868
  434.0 16.4 %copy-start.46 = (s32[8192]{0:T(1024)S(1)}, s32[8192]{0:T(1024)}, u32[]{:S(2)}) copy-start(s32[8192]{0:T(1024)} %copy-done.45) | copy-start | bytes 98308
  434.0 16.4 %copy-start.49 = (f32[8192]{0:T(1024)S(1)}, f32[8192]{0:T(1024)}, u32[]{:S(2)}) copy-start(f32[8192]{0:T(1024)} %copy-done.47) | copy-start | bytes 98308
  434.0 16.4 %copy-start.65 = (f32[8192]{0:T(1024)S(1)}, f32[8192]{0:T(1024)}, u32[]{:S(2)}) copy-start(f32[8192]{0:T(1024)} %copy-done.64) | copy-start | bytes 98308
  450.5 17.3 %copy-start.109 = (pred[3]{0:T(512)(128)(4,1)S(1)}, pred[3]{0:T(512)(128)(4,1)}, u32[]{:S(2)}) copy-start(pred[3]{0:T(512)(128)(4,1)} %copy-done.108) | copy-start | bytes 13
  450.5 17.3 %copy-start.111 = (s32[3]{0:T(128)S(1)}, s32[3]{0:T(128)}, u32[]{:S(2)}) copy-start(s32[3]{0:T(128)} %get-tuple-element.61) | copy-start | bytes 40
  450.5 138.4 %copy-start.44 = (f32[2,3]{0,1:T(4,128)S(1)}, f32[2,3]{0,1:T(4,128)}, u32[]{:S(2)}) copy-start(f32[2,3]{0,1:T(4,128)} %copy-done.43) | copy-start | bytes 76
  450.5 140.0 %copy-start.21 = (f32[1,1,2,8192]{3,2,1,0:T(2,128)S(1)}, f32[1,1,2,8192]{3,2,1,0:T(2,128)}, u32[]{:S(2)}) copy-start(f32[1,1,2,8192]{3,2,1,0:T(2,128)} %param.21) | copy-start | bytes 196612
  450.5 140.0 %copy-start.34 = (f32[1,1,2,8192]{3,2,1,0:T(2,128)S(1)}, f32[1,1,2,8192]{3,2,1,0:T(2,128)}, u32[]{:S(2)}) copy-start(f32[1,1,2,8192]{3,2,1,0:T(2,128)} %param.23) | copy-start | bytes 196612
  450.6 140.0 %copy-start.103 = (f32[2]{0:T(128)S(1)}, f32[2]{0:T(128)}, u32[]{:S(2)}) copy-start(f32[2]{0:T(128)} %get-tuple-element.17) | copy-start | bytes 28
  466.9 128.4 %copy-start.23 = (f32[1,1,2,3,8192]{4,2,3,1,0:T(2,128)S(1)}, f32[1,1,2,3,8192]{4,2,3,1,0:T(2,128)}, u32[]{:S(2)}) copy-start(f32[1,1,2,3,8192]{4,2,3,1,0:T(2,128)} %param.25) | copy-start | bytes 589828
  467.7 252.1 %all-reduce.11.cloned.1.call-start = ((), (), s32[]{:S(2)}) async-start(), calls=%async_computation.3 | async-start | bytes 786432 | tf_op jit(solution)/shard_map/psum | solution.py:282
  750.0 53.1 %copy-start.2 = (f32[19,16,16,128]{3,2,1,0:T(8,128)}, f32[19,16,16,128]{3,2,1,0:T(8,128)S(1)}, u32[]{:S(2)}) copy-start(f32[19,16,16,128]{3,2,1,0:T(8,128)S(1)} %fusion.31) | copy-start | bytes 7471108
  751.1 6.7 collective-permute-start.5
  755.6 7.7 collective-permute-start.4
  775.9 15.3 %collective-permute-start.6 = (f32[19,16,18,1]{0,1,3,2:T(8,128)S(1)}, f32[19,16,18,1]{0,1,3,2:T(8,128)}, u32[]{:S(2)}, u32[]{:S(2)}) collective-permute-start(f32[19,16,18,1]{0,1,3,2:T(8,128)S(1)} %copy.173), channel_id=1, source_target_pairs={{0,1},{1,2},{2,3},{3,4},{4,5},{5,6},{6,7},{7,8},{8,9},{9,10},{10,1... | collective-permute-start | bytes 65672 | tf_op jit(solution)/shard_map/ppermute | solution.py:46
  778.6 7.0 collective-permute-start.7
  (71 other events, 418.0 us)
Sparse Core Ops, SparseCore 0:
  73.4 126.6 all-reduce.4
  206.4 124.3 all-reduce.6
  467.8 121.0 all-reduce.8
  595.4 124.3 all-reduce.10
where the time goes:
time: 827 us; the launch traced here: 819 us
  waiting for transfers between devices  515 us (62%)
  matrix products  147 us (18%)
  local copies, waits for them, and re-layouts  67 us (8%)
  other arithmetic  52.7 us (6%)
  between operations  22.1 us (3%)
  starting transfers between devices  14.5 us (2%)
    psum x2, waiting for transfers between devices, local(): load_rows = lax.psum(row_loads, 'gy')  246 us
    psum x2, waiting for transfers between devices, local(): sampled = lax.psum(samples, 'gy')  244 us
    dot_general x6, matrix products, sample_section(): jnp.dot(across, flattened, precision=lax.Precision.HIGHEST, preferred_ele...  98 us
    dot_general x6, matrix products, spread_section(): lax.dot_general(weighted, across, (((0,), (0,)), ((), ())), precision=lax...  49.3 us
    unnamed x34, other arithmetic  19.7 us
    slice x6, local copies, waits for them, and re-layouts, extended(): lax.slice_in_dim(block, 0, width, axis=dim)  17.4 us
  transfers between devices with their start and end apart: 12, of which 10 were waited for; matrix products, arithmetic and copies ran while one was open for 3% of the time, Pallas kernels for 0%

commit v1 on v0

--- a/solution.py
+++ b/solution.py
@@ -279,7 +279,8 @@
             own_pitch[:, step_index][:, None],
         )
         row_loads = jnp.sum(own_pick[:, :, None, None] * own_loads[:, None], axis=0)
-        load_rows = lax.psum(row_loads, "gy")
+        pieces = lax.all_gather(row_loads, "gy")
+        load_rows = jnp.sum(pieces, axis=0)
         force_field = jnp.zeros((3, levels, x_cells, y_cells), jnp.float32)
         for slot_index in range(row_slots):
             section = spread_section(

time: 827 us -> 680 us (0.82)
  waiting for transfers between devices: 515 us -> 357 us
  other arithmetic: 52.7 us -> 64.3 us
    psum x2 -> x0, waiting for transfers between devices: 246 us -> none  [local(): load_rows = lax.psum(row_loads, 'gy')]
    all_gather x0 -> x2, waiting for transfers between devices: none -> 85.6 us  [local(): pieces = lax.all_gather(row_loads, 'gy')]
  transfers between devices with their start and end apart: 12 -> 12, of which waited for: 10 -> 10; matrix products, arithmetic and copies ran while one was open for 3% -> 4% of each run, Pallas kernels for 0% -> 0%
where the time goes in v1:
time: 680 us; the launch traced here: 670 us
  waiting for transfers between devices  357 us (52%)
  matrix products  146 us (21%)
  local copies, waits for them, and re-layouts  65.6 us (10%)
  other arithmetic  64.3 us (9%)
  between operations  21.7 us (3%)
  starting transfers between devices  15.7 us (2%)
    psum x2, waiting for transfers between devices, local(): sampled = lax.psum(samples, 'gy')  244 us
    dot_general x6, matrix products, sample_section(): jnp.dot(across, flattened, precision=lax.Precision.HIGHEST, preferred_ele...  98.2 us
    all_gather x2, waiting for transfers between devices, local(): pieces = lax.all_gather(row_loads, 'gy')  85.6 us
    dot_general x6, matrix products, spread_section(): lax.dot_general(weighted, across, (((0,), (0,)), ((), ())), precision=lax...  48.2 us
    unnamed x34, other arithmetic  19.7 us
    slice x6, local copies, waits for them, and re-layouts, extended(): lax.slice_in_dim(block, 0, width, axis=dim)  17.5 us
    ppermute x4, waiting for transfers between devices, extended(): lax.ppermute(lax.slice_in_dim(block, 0, width, axis=dim), axis, backward)  16 us
  transfers between devices with their start and end apart: 12, of which 10 were waited for; matrix products, arithmetic and copies ran while one was open for 4% of the time, Pallas kernels for 0%

profile of v1, /device:TPU:27, one launch (start us, length us, event | category | flops | bytes accessed | tf_op | source)
XLA Modules:
  0.0 670.3 jit_solution(5832618063434294344)
XLA Ops:
  16.7 0.8 fusion.240
  22.3 2.4 multiply_reduce_fusion.5
  25.6 16.3 %fusion.50 = f32[8192,3]{0,1:T(4,128)S(1)} fusion(f32[3,16,128]{2,1,0:T(8,128)S(1)} %bitcast.606, f32[]{:T(128)} %bitcast.34, f32[8192]{0:T(1024)S(1)} %get-tuple-element.179, f32[8192]{0:T(1024)S(1)} %get-tuple-element.178, f32[8192]{0:T(1024)S(1)} %get-tuple-element.177, f32[8192]{0:T(1024)S(1)} %get-tuple-element.175, s32[8192]{0:T(1024)S(1)} %get-tuple-element.170, ...), kind=kOutput, calls=%fused_computation.82 | convolution fusion | flops 618373120 | bytes 811524 | tf_op jit(solution)/shard_map/dot_general | solution.py:88
  42.0 16.4 %fusion.44 = f32[8192,3]{0,1:T(4,128)S(1)} fusion(f32[3,16,128]{2,1,0:T(8,128)S(1)} %bitcast.605, f32[]{:T(128)} %bitcast.8, f32[8192]{0:T(1024)S(1)} %get-tuple-element.157, f32[8192]{0:T(1024)S(1)} %get-tuple-element.156, f32[8192]{0:T(1024)S(1)} %get-tuple-element.155, f32[8192]{0:T(1024)S(1)} %get-tuple-element.153, s32[8192]{0:T(1024)S(1)} %get-tuple-element.148, ...), kind=kOutput, calls=%fused_computation.80 | convolution fusion | flops 618373120 | bytes 811524 | tf_op jit(solution)/shard_map/dot_general | solution.py:88
  58.6 16.4 %fusion.47 = f32[8192,3]{0,1:T(4,128)S(1)} fusion(f32[3,16,128]{2,1,0:T(8,128)S(1)} %bitcast.604, f32[]{:T(128)} %bitcast.23, f32[8192]{0:T(1024)S(1)} %copy-done.81, f32[8192]{0:T(1024)S(1)} %copy-done.77, f32[8192]{0:T(1024)S(1)} %copy-done.73, f32[8192]{0:T(1024)S(1)} %copy-done.53, s32[8192]{0:T(1024)S(1)} %copy-done.51, s32[128]{0:T(128)S(1)} %copy-done.130, ...), kind=kOutput, calls=%fused_computation.81 | convolution fusion | flops 618373120 | bytes 811524 | tf_op jit(solution)/shard_map/dot_general | solution.py:88
  75.0 0.8 pad_maximum_fusion.3
  77.6 1.0 fusion.419
  79.6 123.1 %all-reduce.3.cloned.1.call-done = f32[3,3,8192]{2,1,0:T(4,128)} async-done(((f32[3,3,8192]{2,1,0:T(4,128)}), f32[3,3,8192]{2,1,0:T(4,128)}) %all-reduce.3.cloned.1.call-update) | async-done | bytes 294928 | tf_op jit(solution)/shard_map/psum | solution.py:270
  202.7 1.5 multiply_reduce_fusion.9
  204.3 1.4 add_multiply_fusion.17
  205.7 1.4 bitcast_multiply_fusion.3
  207.2 1.6 multiply_reduce_fusion.8
  209.4 1.1 compare_convert_fusion
  210.6 1.2 compare_convert_fusion.1
  211.7 41.9 %all-gather.5.cloned.1.call-done = f32[48,3,8192]{2,1,0:T(4,128)} async-done(((f32[3,3,8192]{2,1,0:T(4,128)}), f32[48,3,8192]{2,1,0:T(4,128)}) %all-gather.5.cloned.1.call-update) | async-done | bytes 4718608 | tf_op jit(solution)/shard_map/all_gather | solution.py:282
  253.7 4.0 reduce_sum.560
  257.9 8.4 %fusion.62 = f32[3,16,128]{2,1,0:T(8,128)S(1)} fusion(f32[]{:T(128)} %bitcast.8, f32[8192]{0:T(1024)S(1)} %copy-done.71, f32[8192]{0:T(1024)S(1)} %copy-done.68, f32[8192]{0:T(1024)S(1)} %copy-done.65, f32[8192]{0:T(1024)S(1)} %copy-done.49, s32[8192]{0:T(1024)S(1)} %get-tuple-element.148, s32[128]{0:T(128)S(1)} %copy-done.130, ...), kind=kOutput, calls=%fused_computation.86 | convolution fusion | flops 618010624 | bytes 811524 | tf_op jit(solution)/shard_map/dot_general | solution.py:101
  266.4 7.9 %fusion.82 = f32[3,16,128]{2,1,0:T(8,128)S(1)} fusion(f32[]{:T(128)} %bitcast.34, f32[8192]{0:T(1024)S(1)} %copy-done.94, f32[8192]{0:T(1024)S(1)} %copy-done.90, f32[8192]{0:T(1024)S(1)} %copy-done.86, f32[8192]{0:T(1024)S(1)} %copy-done.61, s32[8192]{0:T(1024)S(1)} %copy-done.57, s32[128]{0:T(128)S(1)} %copy-done.131, ...), kind=kOutput, calls=%fused_computation.90 | convolution fusion | flops 618010624 | bytes 811524 | tf_op jit(solution)/shard_map/dot_general | solution.py:101
  274.4 8.0 %fusion.72 = f32[3,16,128]{2,1,0:T(8,128)S(1)} fusion(f32[]{:T(128)} %bitcast.23, f32[8192]{0:T(1024)S(1)} %copy-done.82, f32[8192]{0:T(1024)S(1)} %copy-done.78, f32[8192]{0:T(1024)S(1)} %copy-done.74, f32[8192]{0:T(1024)S(1)} %copy-done.54, s32[8192]{0:T(1024)S(1)} %copy-done.51, s32[128]{0:T(128)S(1)} %copy-done.131, ...), kind=kOutput, calls=%fused_computation.88 | convolution fusion | flops 618010624 | bytes 811524 | tf_op jit(solution)/shard_map/dot_general | solution.py:101
  282.9 1.3 copy-done.11
  284.2 2.5 fusion.24
  287.6 4.5 collective-permute-start.1
  292.8 2.5 collective-permute-done.1
  295.3 5.5 collective-permute-done
  301.4 4.5 fusion.415
  305.9 4.1 copy.171
  310.0 4.1 copy.169
  314.1 3.1 collective-permute-start.2
  319.4 4.8 collective-permute-done.3
  324.1 5.9 copy.172
  330.1 5.7 copy.170
  335.8 1.9 constant_dynamic-update-slice_fusion.5
  340.2 1.4 copy-done.8
  344.9 16.4 %fusion.59 = f32[8192,3]{0,1:T(4,128)S(1)} fusion(f32[3,16,128]{2,1,0:T(8,128)S(1)} %bitcast.609, f32[]{:T(128)} %bitcast.34, f32[8192]{0:T(1024)S(1)} %copy-done.95, f32[8192]{0:T(1024)S(1)} %copy-done.91, f32[8192]{0:T(1024)S(1)} %copy-done.87, f32[8192]{0:T(1024)S(1)} %copy-done.62, s32[8192]{0:T(1024)S(1)} %copy-done.58, s32[128]{0:T(128)S(1)} %copy-done.132, ...), kind=kOutput, calls=%fused_computation.85 | convolution fusion | flops 618373120 | bytes 811524 | tf_op jit(solution)/shard_map/dot_general | solution.py:88
  361.4 16.4 %fusion.56 = f32[8192,3]{0,1:T(4,128)S(1)} fusion(f32[3,16,128]{2,1,0:T(8,128)S(1)} %bitcast.608, f32[]{:T(128)} %bitcast.23, f32[8192]{0:T(1024)S(1)} %copy-done.83, f32[8192]{0:T(1024)S(1)} %copy-done.79, f32[8192]{0:T(1024)S(1)} %copy-done.75, f32[8192]{0:T(1024)S(1)} %copy-done.55, s32[8192]{0:T(1024)S(1)} %copy-done.52, s32[128]{0:T(128)S(1)} %copy-done.132, ...), kind=kOutput, calls=%fused_computation.84 | convolution fusion | flops 618373120 | bytes 811524 | tf_op jit(solution)/shard_map/dot_general | solution.py:88
  377.9 16.4 %fusion.53 = f32[8192,3]{0,1:T(4,128)S(1)} fusion(f32[3,16,128]{2,1,0:T(8,128)S(1)} %bitcast.607, f32[]{:T(128)} %bitcast.8, f32[8192]{0:T(1024)S(1)} %copy-done.72, f32[8192]{0:T(1024)S(1)} %copy-done.69, f32[8192]{0:T(1024)S(1)} %copy-done.66, f32[8192]{0:T(1024)S(1)} %copy-done.50, s32[8192]{0:T(1024)S(1)} %copy-done.47, s32[128]{0:T(128)S(1)} %copy-done.132, ...), kind=kOutput, calls=%fused_computation.83 | convolution fusion | flops 618373120 | bytes 811524 | tf_op jit(solution)/shard_map/dot_general | solution.py:88
  394.3 0.8 pad_maximum_fusion.5
  395.2 120.8 %all-reduce.5.cloned.1.call-done = f32[3,3,8192]{2,1,0:T(4,128)} async-done(((f32[3,3,8192]{2,1,0:T(4,128)}), f32[3,3,8192]{2,1,0:T(4,128)}) %all-reduce.5.cloned.1.call-update) | async-done | bytes 294928 | tf_op jit(solution)/shard_map/psum | solution.py:270
  516.0 1.5 multiply_reduce_fusion.7
  517.6 1.8 add_multiply_fusion.15
  519.4 1.4 bitcast_multiply_fusion.2
  520.9 1.6 multiply_reduce_fusion.6
  522.7 1.0 fusion.118
  523.7 43.7 %all-gather.7.cloned.1.call-done = f32[48,3,8192]{2,1,0:T(4,128)} async-done(((f32[3,3,8192]{2,1,0:T(4,128)}), f32[48,3,8192]{2,1,0:T(4,128)}) %all-gather.7.cloned.1.call-update) | async-done | bytes 4718608 | tf_op jit(solution)/shard_map/all_gather | solution.py:282
  567.4 4.0 reduce_sum.596
  571.6 7.9 %fusion.77 = f32[3,16,128]{2,1,0:T(8,128)S(1)} fusion(f32[]{:T(128)} %bitcast.23, f32[8192]{0:T(1024)S(1)} %copy-done.84, f32[8192]{0:T(1024)S(1)} %copy-done.80, f32[8192]{0:T(1024)S(1)} %copy-done.76, f32[8192]{0:T(1024)S(1)} %copy-done.55, s32[8192]{0:T(1024)S(1)} %copy-done.52, s32[128]{0:T(128)S(1)} %copy-done.133, ...), kind=kOutput, calls=%fused_computation.89 | convolution fusion | flops 618010624 | bytes 811524 | tf_op jit(solution)/shard_map/dot_general | solution.py:101
  579.6 7.8 %fusion.87 = f32[3,16,128]{2,1,0:T(8,128)S(1)} fusion(f32[]{:T(128)} %bitcast.34, f32[8192]{0:T(1024)S(1)} %copy-done.96, f32[8192]{0:T(1024)S(1)} %copy-done.92, f32[8192]{0:T(1024)S(1)} %copy-done.88, f32[8192]{0:T(1024)S(1)} %copy-done.63, s32[8192]{0:T(1024)S(1)} %copy-done.59, s32[128]{0:T(128)S(1)} %copy-done.133, ...), kind=kOutput, calls=%fused_computation.91 | convolution fusion | flops 618010624 | bytes 811524 | tf_op jit(solution)/shard_map/dot_general | solution.py:101
  587.5 8.1 %fusion.67 = f32[3,16,128]{2,1,0:T(8,128)S(1)} fusion(f32[]{:T(128)} %bitcast.8, f32[8192]{0:T(1024)S(1)} %copy-done.72, f32[8192]{0:T(1024)S(1)} %copy-done.69, f32[8192]{0:T(1024)S(1)} %copy-done.66, f32[8192]{0:T(1024)S(1)} %copy-done.50, s32[8192]{0:T(1024)S(1)} %copy-done.47, s32[128]{0:T(128)S(1)} %copy-done.133, ...), kind=kOutput, calls=%fused_computation.87 | convolution fusion | flops 618010624 | bytes 811524 | tf_op jit(solution)/shard_map/dot_general | solution.py:101
  596.0 1.3 copy-done.10
  597.4 2.5 fusion.31
  600.1 0.9 slice_dynamic-update-slice_fusion
  601.0 4.5 collective-permute-start.5
  605.6 3.1 collective-permute-done.5
  608.7 5.5 collective-permute-done.4
  614.8 4.5 fusion.414
  619.3 4.1 copy.175
  623.4 3.5 copy.173
  626.9 3.3 collective-permute-start.6
  631.6 5.6 collective-permute-done.7
  637.2 5.7 copy.176
  642.9 5.7 copy.174
  648.6 1.9 maximum_dynamic-update-slice_fusion.5
  654.7 0.8 maximum_dynamic-update-slice_fusion.2
  655.5 1.9 maximum_dynamic-update-slice_fusion.1
  (385 shorter events, 37.0 us)
Async XLA Ops:
  7.2 195.5 %all-reduce.3.cloned.1.call-start = ((), (), s32[]{:S(2)}) async-start(), calls=%async_computation | async-start | bytes 786432 | tf_op jit(solution)/shard_map/psum | solution.py:270
  17.6 240.2 %copy-start.46 = (s32[8192]{0:T(1024)}, s32[8192]{0:T(1024)S(1)}, u32[]{:S(2)}) copy-start(s32[8192]{0:T(1024)S(1)} %get-tuple-element.148) | copy-start | bytes 98308
  17.9 24.1 %copy-start.48 = (f32[8192]{0:T(1024)}, f32[8192]{0:T(1024)S(1)}, u32[]{:S(2)}) copy-start(f32[8192]{0:T(1024)S(1)} %get-tuple-element.153) | copy-start | bytes 98308
  18.2 23.7 %copy-start.60 = (f32[8192]{0:T(1024)}, f32[8192]{0:T(1024)S(1)}, u32[]{:S(2)}) copy-start(f32[8192]{0:T(1024)S(1)} %get-tuple-element.175) | copy-start | bytes 98308
  20.2 21.7 %copy-start.64 = (f32[8192]{0:T(1024)}, f32[8192]{0:T(1024)S(1)}, u32[]{:S(2)}) copy-start(f32[8192]{0:T(1024)S(1)} %get-tuple-element.155) | copy-start | bytes 98308
  20.3 21.7 %copy-start.67 = (f32[8192]{0:T(1024)}, f32[8192]{0:T(1024)S(1)}, u32[]{:S(2)}) copy-start(f32[8192]{0:T(1024)S(1)} %get-tuple-element.156) | copy-start | bytes 98308
  20.3 21.7 %copy-start.70 = (f32[8192]{0:T(1024)}, f32[8192]{0:T(1024)S(1)}, u32[]{:S(2)}) copy-start(f32[8192]{0:T(1024)S(1)} %get-tuple-element.157) | copy-start | bytes 98308
  20.4 21.5 %copy-start.85 = (f32[8192]{0:T(1024)}, f32[8192]{0:T(1024)S(1)}, u32[]{:S(2)}) copy-start(f32[8192]{0:T(1024)S(1)} %get-tuple-element.177) | copy-start | bytes 98308
  20.4 21.5 %copy-start.89 = (f32[8192]{0:T(1024)}, f32[8192]{0:T(1024)S(1)}, u32[]{:S(2)}) copy-start(f32[8192]{0:T(1024)S(1)} %get-tuple-element.178) | copy-start | bytes 98308
  20.4 21.5 %copy-start.93 = (f32[8192]{0:T(1024)}, f32[8192]{0:T(1024)S(1)}, u32[]{:S(2)}) copy-start(f32[8192]{0:T(1024)S(1)} %get-tuple-element.179) | copy-start | bytes 98308
  25.1 241.2 %copy-start.28 = (f32[8192,16]{0,1:T(8,128)}, f32[8192,16]{0,1:T(8,128)S(1)}, u32[]{:S(2)}) copy-start(f32[8192,16]{0,1:T(8,128)S(1)} %select_add_fusion) | copy-start | bytes 1572868
  25.3 232.5 %copy-start.26 = (f32[8192,16]{0,1:T(8,128)}, f32[8192,16]{0,1:T(8,128)S(1)}, u32[]{:S(2)}) copy-start(f32[8192,16]{0,1:T(8,128)S(1)} %select_add_fusion.2) | copy-start | bytes 1572868
  25.5 32.9 %copy-start.31 = (f32[8192,16]{0,1:T(8,128)}, f32[8192,16]{0,1:T(8,128)S(1)}, u32[]{:S(2)}) copy-start(f32[8192,16]{0,1:T(8,128)S(1)} %select_add_fusion.1) | copy-start | bytes 1572868
  42.0 16.5 %copy-start.51 = (s32[8192]{0:T(1024)S(1)}, s32[8192]{0:T(1024)}, u32[]{:S(2)}) copy-start(s32[8192]{0:T(1024)} %get-tuple-element.159) | copy-start | bytes 98308
  42.0 16.5 %copy-start.53 = (f32[8192]{0:T(1024)S(1)}, f32[8192]{0:T(1024)}, u32[]{:S(2)}) copy-start(f32[8192]{0:T(1024)} %get-tuple-element.164) | copy-start | bytes 98308
  42.0 16.5 %copy-start.73 = (f32[8192]{0:T(1024)S(1)}, f32[8192]{0:T(1024)}, u32[]{:S(2)}) copy-start(f32[8192]{0:T(1024)} %get-tuple-element.166) | copy-start | bytes 98308
  42.0 16.5 %copy-start.77 = (f32[8192]{0:T(1024)S(1)}, f32[8192]{0:T(1024)}, u32[]{:S(2)}) copy-start(f32[8192]{0:T(1024)} %get-tuple-element.167) | copy-start | bytes 98308
  42.0 16.5 %copy-start.81 = (f32[8192]{0:T(1024)S(1)}, f32[8192]{0:T(1024)}, u32[]{:S(2)}) copy-start(f32[8192]{0:T(1024)} %get-tuple-element.168) | copy-start | bytes 98308
  42.0 16.5 %copy-start.130 = (s32[128]{0:T(128)S(1)}, s32[128]{0:T(128)}, u32[]{:S(2)}) copy-start(s32[128]{0:T(128)} %iota_add_fusion) | copy-start | bytes 1540
  58.5 18.2 %copy-start.119 = (s32[3]{0:T(128)S(1)}, s32[3]{0:T(128)}, u32[]{:S(2)}) copy-start(s32[3]{0:T(128)} %copy-done.118) | copy-start | bytes 40
  58.5 18.2 %copy-start.128 = (s32[40,2]{0,1:T(2,128)S(1)}, s32[40,2]{0,1:T(2,128)}, u32[]{:S(2)}) copy-start(s32[40,2]{0,1:T(2,128)} %param.20) | copy-start | bytes 964
  58.5 19.1 %copy-start.43 = (f32[1,1,2,8192]{3,2,1,0:T(2,128)S(1)}, f32[1,1,2,8192]{3,2,1,0:T(2,128)}, u32[]{:S(2)}) copy-start(f32[1,1,2,8192]{3,2,1,0:T(2,128)} %param.24) | copy-start | bytes 196612
  58.5 20.0 %copy-start.120 = (s32[3]{0:T(128)S(1)}, s32[3]{0:T(128)}, u32[]{:S(2)}) copy-start(s32[3]{0:T(128)} %get-tuple-element.61) | copy-start | bytes 40
  58.5 145.6 %copy-start.22 = (f32[1,1,2,3,8192]{4,2,3,1,0:T(2,128)S(1)}, f32[1,1,2,3,8192]{4,2,3,1,0:T(2,128)}, u32[]{:S(2)}) copy-start(f32[1,1,2,3,8192]{4,2,3,1,0:T(2,128)} %param.25) | copy-start | bytes 589828
  58.6 145.8 %copy-start.19 = (f32[1,1,2,8192]{3,2,1,0:T(2,128)S(1)}, f32[1,1,2,8192]{3,2,1,0:T(2,128)}, u32[]{:S(2)}) copy-start(f32[1,1,2,8192]{3,2,1,0:T(2,128)} %param.22) | copy-start | bytes 196612
  58.6 145.8 %copy-start.20 = (f32[1,1,2,8192]{3,2,1,0:T(2,128)S(1)}, f32[1,1,2,8192]{3,2,1,0:T(2,128)}, u32[]{:S(2)}) copy-start(f32[1,1,2,8192]{3,2,1,0:T(2,128)} %param.21) | copy-start | bytes 196612
  58.6 145.8 %copy-start.34 = (f32[1,1,2,8192]{3,2,1,0:T(2,128)S(1)}, f32[1,1,2,8192]{3,2,1,0:T(2,128)}, u32[]{:S(2)}) copy-start(f32[1,1,2,8192]{3,2,1,0:T(2,128)} %param.23) | copy-start | bytes 196612
  75.9 177.8 %all-gather.5.cloned.1.call-start = ((), (), s32[]{:S(2)}) async-start(), calls=%async_computation.2 | async-start | bytes 6684672 | tf_op jit(solution)/shard_map/all_gather | solution.py:282
  78.7 179.0 %copy-start.44 = (f32[2,3]{0,1:T(4,128)}, f32[2,3]{0,1:T(4,128)S(1)}, u32[]{:S(2)}) copy-start(f32[2,3]{0,1:T(4,128)S(1)} %copy.166) | copy-start | bytes 76
  208.8 307.2 %all-reduce.5.cloned.1.call-start = ((), (), s32[]{:S(2)}) async-start(), calls=%async_computation.1 | async-start | bytes 786432 | tf_op jit(solution)/shard_map/psum | solution.py:270
  209.4 73.1 %copy-start.122 = (f32[16]{0:T(128)}, f32[16]{0:T(128)S(1)}, u32[]{:S(2)}) copy-start(f32[16]{0:T(128)S(1)} %compare_convert_fusion.2) | copy-start | bytes 196
  287.6 7.7 %collective-permute-start.1 = (f32[19,16,1,128]{3,2,1,0:T(1,128)S(1)}, f32[19,16,1,128]{3,2,1,0:T(1,128)S(1)}, u32[]{:S(2)}, u32[]{:S(2)}) collective-permute-start(f32[19,16,1,128]{3,2,1,0:T(1,128)S(1)} %get-tuple-element.115), channel_id=1, source_target_pairs={{16,0},{32,16},{48,32},{64,48},{80,64},{96,80},{112,96},{128,112},... | collective-permute-start | bytes 466952 | tf_op jit(solution)/shard_map/ppermute | solution.py:49
  292.2 8.6 %collective-permute-start = (f32[19,16,1,128]{3,2,1,0:T(1,128)S(1)}, f32[19,16,1,128]{3,2,1,0:T(1,128)S(1)}, u32[]{:S(2)}, u32[]{:S(2)}) collective-permute-start(f32[19,16,1,128]{3,2,1,0:T(1,128)S(1)} %get-tuple-element.116), channel_id=1, source_target_pairs={{0,16},{16,32},{32,48},{48,64},{64,80},{80,96},{96,112},{112,128},... | collective-permute-start | bytes 466952 | tf_op jit(solution)/shard_map/ppermute | solution.py:46
  292.8 50.3 %copy-start.36 = (f32[1,16,128]{2,1,0:T(8,128)}, f32[1,16,128]{2,1,0:T(8,128)S(1)}, u32[]{:S(2)}) copy-start(f32[1,16,128]{2,1,0:T(8,128)S(1)} %get-tuple-element.106) | copy-start | bytes 24580
  314.1 16.0 %collective-permute-start.2 = (f32[19,16,18,1]{0,1,3,2:T(8,128)}, f32[19,16,18,1]{0,1,3,2:T(8,128)}, u32[]{:S(2)}, u32[]{:S(2)}) collective-permute-start(f32[19,16,18,1]{0,1,3,2:T(8,128)} %copy.169), channel_id=1, source_target_pairs={{0,1},{1,2},{2,3},{3,4},{4,5},{5,6},{6,7},{7,8},{8,9},{9,10},{10,1... | collective-permute-start | bytes 65672 | tf_op jit(solution)/shard_map/ppermute | solution.py:46
  317.2 7.0 %collective-permute-start.3 = (f32[19,16,18,1]{0,1,3,2:T(8,128)}, f32[19,16,18,1]{0,1,3,2:T(8,128)}, u32[]{:S(2)}, u32[]{:S(2)}) collective-permute-start(f32[19,16,18,1]{0,1,3,2:T(8,128)} %copy.171), channel_id=1, source_target_pairs={{1,0},{2,1},{3,2},{4,3},{5,4},{6,5},{7,6},{8,7},{9,8},{10,9},{11,1... | collective-permute-start | bytes 65672 | tf_op jit(solution)/shard_map/ppermute | solution.py:49
  317.9 25.2 %copy-start.14 = (f32[15,16,128]{2,1,0:T(8,128)}, f32[15,16,128]{2,1,0:T(8,128)S(1)}, u32[]{:S(2)}) copy-start(f32[15,16,128]{2,1,0:T(8,128)S(1)} %get-tuple-element.85) | copy-start | bytes 368644
  343.3 18.0 %copy-start.9 = (f32[19,16,16,128]{3,2,1,0:T(8,128)}, f32[19,16,16,128]{3,2,1,0:T(8,128)S(1)}, u32[]{:S(2)}) copy-start(f32[19,16,16,128]{3,2,1,0:T(8,128)S(1)} %fusion.145) | copy-start | bytes 7471108
  343.9 17.3 %copy-start.12 = (f32[16,16,128]{2,1,0:T(8,128)}, f32[16,16,128]{2,1,0:T(8,128)S(1)}, u32[]{:S(2)}) copy-start(f32[16,16,128]{2,1,0:T(8,128)S(1)} %get-tuple-element.12) | copy-start | bytes 393220
  344.8 16.4 %copy-start.33 = (f32[8192,16]{0,1:T(8,128)S(1)}, f32[8192,16]{0,1:T(8,128)}, u32[]{:S(2)}) copy-start(f32[8192,16]{0,1:T(8,128)} %copy-done.31) | copy-start | bytes 1572868
  344.8 16.4 %copy-start.52 = (s32[8192]{0:T(1024)S(1)}, s32[8192]{0:T(1024)}, u32[]{:S(2)}) copy-start(s32[8192]{0:T(1024)} %get-tuple-element.159) | copy-start | bytes 98308
  344.8 16.4 %copy-start.55 = (f32[8192]{0:T(1024)S(1)}, f32[8192]{0:T(1024)}, u32[]{:S(2)}) copy-start(f32[8192]{0:T(1024)} %get-tuple-element.164) | copy-start | bytes 98308
  344.9 16.4 %copy-start.75 = (f32[8192]{0:T(1024)S(1)}, f32[8192]{0:T(1024)}, u32[]{:S(2)}) copy-start(f32[8192]{0:T(1024)} %get-tuple-element.166) | copy-start | bytes 98308
  344.9 16.4 %copy-start.79 = (f32[8192]{0:T(1024)S(1)}, f32[8192]{0:T(1024)}, u32[]{:S(2)}) copy-start(f32[8192]{0:T(1024)} %get-tuple-element.167) | copy-start | bytes 98308
  344.9 16.4 %copy-start.83 = (f32[8192]{0:T(1024)S(1)}, f32[8192]{0:T(1024)}, u32[]{:S(2)}) copy-start(f32[8192]{0:T(1024)} %get-tuple-element.168) | copy-start | bytes 98308
  361.3 16.4 %copy-start.27 = (f32[8192,16]{0,1:T(8,128)S(1)}, f32[8192,16]{0,1:T(8,128)}, u32[]{:S(2)}) copy-start(f32[8192,16]{0,1:T(8,128)} %copy-done.26) | copy-start | bytes 1572868
  361.3 16.4 %copy-start.47 = (s32[8192]{0:T(1024)S(1)}, s32[8192]{0:T(1024)}, u32[]{:S(2)}) copy-start(s32[8192]{0:T(1024)} %copy-done.46) | copy-start | bytes 98308
  361.4 16.4 %copy-start.50 = (f32[8192]{0:T(1024)S(1)}, f32[8192]{0:T(1024)}, u32[]{:S(2)}) copy-start(f32[8192]{0:T(1024)} %copy-done.48) | copy-start | bytes 98308
  361.4 16.4 %copy-start.66 = (f32[8192]{0:T(1024)S(1)}, f32[8192]{0:T(1024)}, u32[]{:S(2)}) copy-start(f32[8192]{0:T(1024)} %copy-done.64) | copy-start | bytes 98308
  361.4 16.4 %copy-start.69 = (f32[8192]{0:T(1024)S(1)}, f32[8192]{0:T(1024)}, u32[]{:S(2)}) copy-start(f32[8192]{0:T(1024)} %copy-done.67) | copy-start | bytes 98308
  361.4 16.4 %copy-start.72 = (f32[8192]{0:T(1024)S(1)}, f32[8192]{0:T(1024)}, u32[]{:S(2)}) copy-start(f32[8192]{0:T(1024)} %copy-done.70) | copy-start | bytes 98308
  377.8 138.2 %copy-start.45 = (f32[2,3]{0,1:T(4,128)S(1)}, f32[2,3]{0,1:T(4,128)}, u32[]{:S(2)}) copy-start(f32[2,3]{0,1:T(4,128)} %copy-done.44) | copy-start | bytes 76
  377.8 139.8 %copy-start.21 = (f32[1,1,2,8192]{3,2,1,0:T(2,128)S(1)}, f32[1,1,2,8192]{3,2,1,0:T(2,128)}, u32[]{:S(2)}) copy-start(f32[1,1,2,8192]{3,2,1,0:T(2,128)} %param.21) | copy-start | bytes 196612
  377.8 139.8 %copy-start.35 = (f32[1,1,2,8192]{3,2,1,0:T(2,128)S(1)}, f32[1,1,2,8192]{3,2,1,0:T(2,128)}, u32[]{:S(2)}) copy-start(f32[1,1,2,8192]{3,2,1,0:T(2,128)} %param.23) | copy-start | bytes 196612
  377.9 139.8 %copy-start.111 = (f32[2]{0:T(128)S(1)}, f32[2]{0:T(128)}, u32[]{:S(2)}) copy-start(f32[2]{0:T(128)} %get-tuple-element.17) | copy-start | bytes 28
  394.3 128.3 %copy-start.117 = (pred[3]{0:T(512)(128)(4,1)S(1)}, pred[3]{0:T(512)(128)(4,1)}, u32[]{:S(2)}) copy-start(pred[3]{0:T(512)(128)(4,1)} %copy-done.116) | copy-start | bytes 13
  394.3 128.3 %copy-start.121 = (s32[3]{0:T(128)S(1)}, s32[3]{0:T(128)}, u32[]{:S(2)}) copy-start(s32[3]{0:T(128)} %get-tuple-element.61) | copy-start | bytes 40
  394.3 128.4 %copy-start.23 = (f32[1,1,2,3,8192]{4,2,3,1,0:T(2,128)S(1)}, f32[1,1,2,3,8192]{4,2,3,1,0:T(2,128)}, u32[]{:S(2)}) copy-start(f32[1,1,2,3,8192]{4,2,3,1,0:T(2,128)} %param.25) | copy-start | bytes 589828
  395.2 172.2 %all-gather.7.cloned.1.call-start = ((), (), s32[]{:S(2)}) async-start(), calls=%async_computation.3 | async-start | bytes 6684672 | tf_op jit(solution)/shard_map/all_gather | solution.py:282
  599.9 54.8 %copy-start.2 = (f32[19,16,16,128]{3,2,1,0:T(8,128)}, f32[19,16,16,128]{3,2,1,0:T(8,128)S(1)}, u32[]{:S(2)}) copy-start(f32[19,16,16,128]{3,2,1,0:T(8,128)S(1)} %fusion.31) | copy-start | bytes 7471108
  601.0 7.7 %collective-permute-start.5 = (f32[19,16,1,128]{3,2,1,0:T(1,128)S(1)}, f32[19,16,1,128]{3,2,1,0:T(1,128)S(1)}, u32[]{:S(2)}, u32[]{:S(2)}) collective-permute-start(f32[19,16,1,128]{3,2,1,0:T(1,128)S(1)} %get-tuple-element.100), channel_id=1, source_target_pairs={{16,0},{32,16},{48,32},{64,48},{80,64},{96,80},{112,96},{128,112},... | collective-permute-start | bytes 466952 | tf_op jit(solution)/shard_map/ppermute | solution.py:49
  605.6 8.6 %collective-permute-start.4 = (f32[19,16,1,128]{3,2,1,0:T(1,128)S(1)}, f32[19,16,1,128]{3,2,1,0:T(1,128)S(1)}, u32[]{:S(2)}, u32[]{:S(2)}) collective-permute-start(f32[19,16,1,128]{3,2,1,0:T(1,128)S(1)} %get-tuple-element.101), channel_id=1, source_target_pairs={{0,16},{16,32},{32,48},{48,64},{64,80},{80,96},{96,112},{112,128},... | collective-permute-start | bytes 466952 | tf_op jit(solution)/shard_map/ppermute | solution.py:46
  626.9 16.0 %collective-permute-start.6 = (f32[19,16,18,1]{0,1,3,2:T(8,128)S(1)}, f32[19,16,18,1]{0,1,3,2:T(8,128)}, u32[]{:S(2)}, u32[]{:S(2)}) collective-permute-start(f32[19,16,18,1]{0,1,3,2:T(8,128)S(1)} %copy.173), channel_id=1, source_target_pairs={{0,1},{1,2},{2,3},{3,4},{4,5},{5,6},{6,7},{7,8},{8,9},{9,10},{10,1... | collective-permute-start | bytes 65672 | tf_op jit(solution)/shard_map/ppermute | solution.py:46
  630.2 7.0 %collective-permute-start.7 = (f32[19,16,18,1]{0,1,3,2:T(8,128)}, f32[19,16,18,1]{0,1,3,2:T(8,128)}, u32[]{:S(2)}, u32[]{:S(2)}) collective-permute-start(f32[19,16,18,1]{0,1,3,2:T(8,128)} %copy.175), channel_id=1, source_target_pairs={{1,0},{2,1},{3,2},{4,3},{5,4},{6,5},{7,6},{8,7},{9,8},{10,9},{11,1... | collective-permute-start | bytes 65672 | tf_op jit(solution)/shard_map/ppermute | solution.py:49
  (82 other events, 460.1 us)
Sparse Core Ops, SparseCore 0:
  76.0 126.6 all-reduce.2
  209.0 44.6 all-gather.4
  395.3 120.6 all-reduce.4
  522.7 44.6 all-gather.6
